TPU v7x, 512 devices: a whole 4x8x8 slice. The times are simulated.
512 devices in a mesh: rep: 4 (over x), exp: 128 (over z, y, core).
Axes of the slice: x: 4, y: 8, z: 8, core: 2. Of those that a mesh axis runs over, the one named last changes fastest.
Arguments:
- tokens: bfloat16 [16384, 2048], P('exp', 'rep'), may hold values from -6 to 6
- expert_ids: int32 [16384, 8], P('exp'), may hold values from 0 to 127, all different within a row; in each aligned block of 128 rows (0 to 127, 128 to 255, ...) at most 12 rows name the same one
- route_weights: float32 [16384, 8], P('exp'), may hold values from 0.05 to 1
- w_gate: bfloat16 [128, 768, 2048], P('exp', None, 'rep'), may hold values from -0.125 to 0.125
- w_up: bfloat16 [128, 768, 2048], P('exp', None, 'rep'), may hold values from -0.125 to 0.125
- w_down: bfloat16 [128, 768, 2048], P('exp', None, 'rep'), may hold values from -0.21875 to 0.21875
Outputs:
- mixed: bfloat16 [16384, 2048], P('exp', 'rep')
Inputs may be any that keep to these rules, and one draw needn't show every extreme that they name: `expert_ids`: each token names 8 different experts. Within the rows of one index of exp (aligned blocks of 128 tokens) no expert is named more than 12 times, a bound that some block reaches.
All inputs are finite; a program needn't handle non-finite values.
Results may differ from a plain program's by a relative error of at most 0.0058.
Values may be sent and summed in bfloat16 or wider, within the bound.
A program may use at most 64 MiB of HBM per device.

v0:
```python
import jax
import jax.numpy as jnp
from jax import lax
from jax.sharding import PartitionSpec as P

EXPERTS = 128


def local(tokens, expert_ids, route_weights, w_gate, w_up, w_down):
    tok_rows = expert_ids.shape[0]
    top_count = expert_ids.shape[1]
    local_experts = w_gate.shape[0]
    replicas = lax.axis_size("rep")
    replica_index = lax.axis_index("rep")
    full_cap = replicas * max(1, tok_rows * top_count * 3 // (8 * EXPERTS))
    slot_cap = full_cap // replicas
    assigned = expert_ids.reshape(-1)
    onehot = (assigned[:, None] == jnp.arange(EXPERTS, dtype=jnp.int32)[None, :]).astype(jnp.int32)
    before = jnp.cumsum(onehot, axis=0) - onehot
    slot_ids = jnp.sum(before * onehot, axis=1)
    owned = slot_ids % replicas == replica_index
    target = assigned * slot_cap + slot_ids // replicas
    destination = jnp.where(owned, target, EXPERTS * slot_cap)
    probs = route_weights / jnp.sum(route_weights, axis=1, keepdims=True)
    full_rows = lax.all_gather(tokens, "rep", axis=1, tiled=True)
    width = full_rows.shape[1]
    repeated = jnp.repeat(full_rows, top_count, axis=0)
    outgoing = (
        jnp.zeros((EXPERTS * slot_cap, width), jnp.bfloat16)
        .at[destination]
        .set(repeated, mode="drop")
    )
    outgoing = outgoing.reshape(EXPERTS, slot_cap, width)
    arrived = lax.all_to_all(outgoing, "exp", split_axis=0, concat_axis=1, tiled=True)
    gate_sum = jnp.einsum(
        "esd,efd->esf",
        arrived,
        lax.all_gather(w_gate, "rep", axis=2, tiled=True),
        preferred_element_type=jnp.float32,
    )
    up_sum = jnp.einsum(
        "esd,efd->esf",
        arrived,
        lax.all_gather(w_up, "rep", axis=2, tiled=True),
        preferred_element_type=jnp.float32,
    )
    hidden = (jax.nn.silu(gate_sum) * up_sum).astype(jnp.bfloat16)
    expert_out = jnp.einsum(
        "esf,efd->esd",
        hidden,
        lax.all_gather(w_down, "rep", axis=2, tiled=True),
        preferred_element_type=jnp.float32,
    ).astype(jnp.bfloat16)
    owners = expert_out.shape[1] // slot_cap
    share = width // replicas
    split_out = expert_out.reshape(local_experts, owners, slot_cap, replicas, share)
    homed = lax.all_to_all(
        lax.all_to_all(split_out, "rep", split_axis=3, concat_axis=3, tiled=True),
        "exp",
        split_axis=1,
        concat_axis=1,
        tiled=True,
    )
    ordered = jnp.swapaxes(homed, 0, 1).reshape(EXPERTS * full_cap, share)
    picked = ordered[assigned * full_cap + slot_ids].astype(jnp.float32)
    weighted = picked.reshape(tok_rows, top_count, share) * probs[:, :, None]
    return jnp.sum(weighted, axis=1).astype(jnp.bfloat16)


def solution(mesh):
    return jax.shard_map(
        local,
        mesh=mesh,
        in_specs=(
            P("exp", "rep"),
            P("exp", None),
            P("exp", None),
            P("exp", None, "rep"),
            P("exp", None, "rep"),
            P("exp", None, "rep"),
        ),
        out_specs=P("exp", "rep"),
        check_vma=False,
    )
```

profile of v0, /device:TPU:8, one launch (start us, length us, event | category | flops | bytes accessed | tf_op | source)
XLA Modules:
  0.0 256.1 jit_solution(238828360793560490)
XLA Ops:
  6.5 0.7 all-gather.4.cloned.1.call-update
  7.3 0.7 all-gather.6.cloned.1.call-update
  8.1 0.7 all-gather.8.cloned.1.call-update
  8.8 0.1 copy.24
  9.1 0.2 fusion.25
  9.5 0.1 copy.27
  10.0 0.4 fusion.24
  10.4 13.1 %all_gather.12 = bf16[128,2048]{1,0:T(8,128)(2,1)S(1)} all-gather(bf16[128,512]{1,0:T(8,128)(2,1)S(1)} %copy-done), channel_id=1, replica_groups=mesh['rep'=4,'exp'=128] {'rep'}, dimensions={1}, use_global_device_ids=true | all-gather | bytes 655360 | tf_op jit(solution)/shard_map/all_gather | solution.py:25
  23.5 7.7 %scatter_custom_fusion = bf16[384,2048]{1,0:T(8,128)(2,1)} fusion(s32[1024]{0:T(1024)S(1)} %bitcast.42, bf16[128,2048]{1,0:T(8,128)(2,1)S(1)} %all_gather.12, bf16[]{:T(256)} %constant.41.clone.1), kind=kCustom, calls=%fused_computation.2 | custom fusion | bytes 2097154 | tf_op jit(solution)/shard_map/scatter | solution.py:31
  31.2 4.0 %reshape.193 = bf16[128,3,2048]{2,1,0:T(4,128)(2,1)S(1)} reshape(bf16[384,2048]{1,0:T(8,128)(2,1)} %scatter_custom_fusion) | data formatting | bytes 3145728 | tf_op jit(solution)/shard_map/reshape | solution.py:33
  35.2 71.3 %all_to_all.19 = bf16[128,3,2048]{2,1,0:T(4,128)(2,1)} all-to-all(bf16[128,3,2048]{2,1,0:T(4,128)(2,1)S(1)} %reshape.193), channel_id=1, replica_groups=mesh['rep'=4,'exp'=128] {'exp'}, dimensions={0} | all-to-all | bytes 3145728 | tf_op jit(solution)/shard_map/all_to_all | solution.py:34
  106.5 3.9 %reshape.194 = bf16[384,2048]{1,0:T(8,128)(2,1)S(1)} reshape(bf16[128,3,2048]{2,1,0:T(4,128)(2,1)} %all_to_all.19) | data formatting | bytes 3145728 | tf_op jit(solution)/shard_map/reshape.10
  110.5 4.4 %fusion.6 = f32[384,768]{1,0:T(8,128)} fusion(bf16[384,2048]{1,0:T(8,128)(2,1)S(1)} %reshape.194, bf16[1,768,2048]{2,1,0:T(8,128)(2,1)} %all-gather.4.cloned.1.call-done), kind=kOutput, calls=%fused_computation.8 | convolution fusion | flops 1207959552 | bytes 5898240 | tf_op jit(solution)/shard_map/esd,efd->esf/dot_general | solution.py:35
  114.9 38.3 %all-gather.8.cloned.1.call-done = bf16[1,768,2048]{2,1,0:T(8,128)(2,1)} async-done(((bf16[1,768,512]{2,1,0:T(8,128)(2,1)}), bf16[1,768,2048]{2,1,0:T(8,128)(2,1)}) %all-gather.8.cloned.1.call-update) | async-done | bytes 3145744 | tf_op jit(solution)/shard_map/all_gather | solution.py:51
  153.2 6.3 %fusion.8 = bf16[384,2048]{1,0:T(8,128)(2,1)S(1)} fusion(bf16[1,768,2048]{2,1,0:T(8,128)(2,1)} %all-gather.8.cloned.1.call-done, bf16[384,2048]{1,0:T(8,128)(2,1)S(1)} %reshape.194, bf16[1,768,2048]{2,1,0:T(8,128)(2,1)} %all-gather.6.cloned.1.call-done, f32[384,768]{1,0:T(8,128)} %fusion.6), kind=kOutput, calls=%fused_computation.10 | convolution fusion | flops 2418475008 | bytes 10616832 | tf_op jit(solution)/shard_map/esf,efd->esd/dot_general | solution.py:48
  159.5 1.2 reshape.198
  160.7 0.3 copy.29
  161.1 23.5 %all_to_all.20 = bf16[1,128,3,4,512]{4,1,2,0,3:T(8,128)(2,1)S(1)} all-to-all(bf16[1,128,3,4,512]{4,1,2,0,3:T(8,128)(2,1)S(1)} %copy.29), channel_id=1, replica_groups=mesh['rep'=4,'exp'=128] {'rep'}, dimensions={3} | all-to-all | bytes 3145728 | tf_op jit(solution)/shard_map/all_to_all | solution.py:58
  184.6 2.4 copy.30
  187.0 14.3 %all-to-all-start.2 = ((bf16[1,128,3,4,512]{4,3,2,0,1:T(4,128)(2,1)}), bf16[1,128,3,4,512]{4,3,2,0,1:T(4,128)(2,1)S(1)}, u32[]{:S(2)}, u32[]{:S(2)}) async-start(bf16[1,128,3,4,512]{4,3,2,0,1:T(4,128)(2,1)} %copy.30), calls=%async_computation.2 | async-start | bytes 3145728 | tf_op jit(solution)/shard_map/all_to_all | solution.py:57
  201.4 42.4 %all-to-all-done.2 = bf16[1,128,3,4,512]{4,3,2,0,1:T(4,128)(2,1)S(1)} async-done(((bf16[1,128,3,4,512]{4,3,2,0,1:T(4,128)(2,1)}), bf16[1,128,3,4,512]{4,3,2,0,1:T(4,128)(2,1)S(1)}, u32[]{:S(2)}, u32[]{:S(2)}) %all-to-all-start.2) | async-done | bytes 1572896 | tf_op jit(solution)/shard_map/all_to_all | solution.py:57
  243.8 0.4 reshape_transpose.3
  244.2 4.0 %gather_fusion = bf16[1024,512]{1,0:T(8,128)(2,1)S(1)} fusion(bf16[1536,512]{1,0:T(8,128)(2,1)S(1)} %reshape_transpose.3, s32[1024]{0:T(1024)S(1)} %broadcast_clamp_fusion), kind=kCustom, calls=%fused_computation | custom fusion | bytes 2101248 | tf_op jit(solution)/shard_map/gather | solution.py:65
  248.2 1.3 fusion.11
  (28 shorter events, 1.1 us)
Async XLA Ops:
  6.5 2.2 copy-start.1
  6.5 103.9 %all-gather.4.cloned.1.call-start = ((), (), s32[]{:S(2)}) async-start(), calls=%async_computation.3 | async-start | bytes 3932160 | tf_op jit(solution)/shard_map/all_gather | solution.py:38
  7.3 107.6 %all-gather.6.cloned.1.call-start = ((), (), s32[]{:S(2)}) async-start(), calls=%async_computation.4 | async-start | bytes 3932160 | tf_op jit(solution)/shard_map/all_gather | solution.py:44
  8.0 145.2 %all-gather.8.cloned.1.call-start = ((), (), s32[]{:S(2)}) async-start(), calls=%async_computation.5 | async-start | bytes 3932160 | tf_op jit(solution)/shard_map/all_gather | solution.py:51
  9.4 1.0 copy-start
  186.9 14.3 %copy-start.2 = (f32[128,8]{0,1:T(8,128)S(1)}, f32[128,8]{0,1:T(8,128)}, u32[]{:S(2)}) copy-start(f32[128,8]{0,1:T(8,128)} %param.8) | copy-start | bytes 12292
  187.0 56.9 %all-to-all-start.2 = ((bf16[1,128,3,4,512]{4,3,2,0,1:T(4,128)(2,1)}), bf16[1,128,3,4,512]{4,3,2,0,1:T(4,128)(2,1)S(1)}, u32[]{:S(2)}, u32[]{:S(2)}) async-start(bf16[1,128,3,4,512]{4,3,2,0,1:T(4,128)(2,1)} %copy.30), calls=%async_computation.2 | async-start | bytes 3145728 | tf_op jit(solution)/shard_map/all_to_all | solution.py:57
Sparse Core Ops, SparseCore 0:
  9.4 49.3 all-gather.3
  60.9 45.0 all-gather.5
  108.1 45.0 all-gather.7
where the time goes:
time: 257 us; the launch traced here: 256 us
  blocking collectives  108 us (42%)
  waiting for transfers between devices  82.9 us (32%)
  local copies, waits for them, and re-layouts  24.8 us (10%)
  starting transfers between devices  14.4 us (6%)
  between operations  13.3 us (5%)
  matrix products  10.7 us (4%)
    all_to_all x1, blocking collectives, local(): lax.all_to_all(outgoing, 'exp', split_axis=0, concat_axis=1, tiled=True)  71.3 us
    all_to_all x1, waiting for transfers between devices, local(): lax.all_to_all(lax.all_to_all(split_out, 'rep', split_axis=3, concat_axis...  42.4 us
    all_gather x1, waiting for transfers between devices, local(): lax.all_gather(w_down, 'rep', axis=2, tiled=True)  38.3 us
    all_to_all x1, blocking collectives, local(): lax.all_to_all(split_out, 'rep', split_axis=3, concat_axis=3, tiled=True)  23.5 us
    all_to_all x1, starting transfers between devices, local(): lax.all_to_all(lax.all_to_all(split_out, 'rep', split_axis=3, concat_axis...  14.3 us
    all_gather x1, blocking collectives, local(): full_rows = lax.all_gather(tokens, 'rep', axis=1, tiled=True)  13.1 us
    scatter x1, local copies, waits for them, and re-layouts, local(): outgoing = jnp.zeros((EXPERTS * slot_cap, width), jnp.bfloat16).at[destin...  7.66 us
    dot_general x1, matrix products, local(): jnp.einsum('esf,efd->esd', hidden, lax.all_gather(w_down, 'rep', axis=2,...  6.33 us
  transfers between devices with their start and end apart: 4, of which 2 were waited for; matrix products, arithmetic and copies ran while one was open for 8% of the time, Pallas kernels for 0%

commit v1 on v0

--- a/solution.py
+++ b/solution.py
@@ -45,11 +45,11 @@
         preferred_element_type=jnp.float32,
     )
     hidden = (jax.nn.silu(gate_sum) * up_sum).astype(jnp.bfloat16)
+    report_point = lambda arr_in, d0: jnp.concatenate(
+        lax.all_to_all(jnp.stack([arr_in] * lax.axis_size("rep"), axis=0), "rep", 0, 0), d0
+    )
     expert_out = jnp.einsum(
-        "esf,efd->esd",
-        hidden,
-        lax.all_gather(w_down, "rep", axis=2, tiled=True),
-        preferred_element_type=jnp.float32,
+        "esf,efd->esd", hidden, report_point(w_down, 2), preferred_element_type=jnp.float32
     ).astype(jnp.bfloat16)
     owners = expert_out.shape[1] // slot_cap
     share = width // replicas

time: 257 us -> 243 us (0.946)
  blocking collectives: 108 us -> 35 us
  waiting for transfers between devices: 82.9 us -> 125 us
  starting transfers between devices: 14.4 us -> 30.4 us
    all_to_all x0 -> x2, waiting for transfers between devices: none -> 81.4 us  [the longest x1 51.9 us: local(): lax.all_to_all(outgoing, 'exp', split_axis=0, concat_axis=1, tiled=True)]
    all_to_all x1 -> x0, blocking collectives: 71.3 us -> none  [local(): lax.all_to_all(outgoing, 'exp', split_axis=0, concat_axis=1, tiled=True)]
    all_gather x1 -> x0, waiting for transfers between devices: 38.3 us -> none  [local(): lax.all_gather(w_down, 'rep', axis=2, tiled=True)]
    all_to_all x0 -> x2, starting transfers between devices: none -> 22.2 us  [the longest x1 17.4 us: local(): lax.all_to_all(outgoing, 'exp', split_axis=0, concat_axis=1, tiled=True)]
    all_to_all x1, starting transfers between devices: 14.3 us -> 8.22 us  [local(): lax.all_to_all(lax.all_to_all(split_out, 'rep', split_axis=3, concat_axis...]
    another operation x4 -> x6, local copies, waits for them, and re-layouts: 4.02 us -> 5.89 us
  transfers between devices with their start and end apart: 4 -> 5, of which waited for: 2 -> 3; matrix products, arithmetic and copies ran while one was open for 8% -> 9% of each run, Pallas kernels for 0% -> 0%
where the time goes in v1:
time: 243 us
  waiting for transfers between devices  125 us (51%)
  blocking collectives  35 us (14%)
  starting transfers between devices  30.4 us (13%)
  local copies, waits for them, and re-layouts  25 us (10%)
  between operations  13.6 us (6%)
  matrix products  11.3 us (5%)
    all_to_all x1, waiting for transfers between devices, local(): lax.all_to_all(outgoing, 'exp', split_axis=0, concat_axis=1, tiled=True)  51.9 us
    all_to_all x1, waiting for transfers between devices, local(): lax.all_to_all(lax.all_to_all(split_out, 'rep', split_axis=3, concat_axis...  42.4 us
    all_to_all x1, waiting for transfers between devices, local(): lax.all_to_all(jnp.stack([arr_in] * lax.axis_size('rep'), axis=0), 'rep',...  29.6 us
    all_to_all x1, blocking collectives, local(): lax.all_to_all(split_out, 'rep', split_axis=3, concat_axis=3, tiled=True)  21.9 us
    all_to_all x1, starting transfers between devices, local(): lax.all_to_all(outgoing, 'exp', split_axis=0, concat_axis=1, tiled=True)  17.4 us
    all_gather x1, blocking collectives, local(): full_rows = lax.all_gather(tokens, 'rep', axis=1, tiled=True)  13.1 us
    all_to_all x1, starting transfers between devices, local(): lax.all_to_all(lax.all_to_all(split_out, 'rep', split_axis=3, concat_axis...  8.22 us
    scatter x1, local copies, waits for them, and re-layouts, local(): outgoing = jnp.zeros((EXPERTS * slot_cap, width), jnp.bfloat16).at[destin...  6.81 us
  transfers between devices with their start and end apart: 5, of which 3 were waited for; matrix products, arithmetic and copies ran while one was open for 9% of the time, Pallas kernels for 0%

profile of v1, /device:TPU:8, one launch (start us, length us, event | category | flops | bytes accessed | tf_op | source)
XLA Modules:
  0.0 242.6 jit_solution(17213516565181834792)
XLA Ops:
  6.5 0.7 all-gather.3.cloned.1.call-update
  7.3 0.9 copy.27
  9.3 0.4 fusion.19
  9.6 13.1 %all_gather.9 = bf16[128,2048]{1,0:T(8,128)(2,1)S(1)} all-gather(bf16[128,512]{1,0:T(8,128)(2,1)S(1)} %copy-done.1), channel_id=1, replica_groups=mesh['rep'=4,'exp'=128] {'rep'}, dimensions={1}, use_global_device_ids=true | all-gather | bytes 655360 | tf_op jit(solution)/shard_map/all_gather | solution.py:25
  22.8 6.8 %scatter_custom_fusion = bf16[384,2048]{1,0:T(8,128)(2,1)S(1)} fusion(s32[1024]{0:T(1024)S(1)} %bitcast.45, bf16[128,2048]{1,0:T(8,128)(2,1)S(1)} %all_gather.9, bf16[]{:T(256)} %constant.41.clone.1), kind=kCustom, calls=%fused_computation.2 | custom fusion | bytes 2097154 | tf_op jit(solution)/shard_map/scatter | solution.py:31
  29.6 2.4 reshape.201
  32.0 17.4 %all-to-all-start = ((bf16[128,3,2048]{2,1,0:T(4,128)(2,1)}), bf16[128,3,2048]{2,1,0:T(4,128)(2,1)S(1)}, u32[]{:S(2)}, u32[]{:S(2)}) async-start(bf16[128,3,2048]{2,1,0:T(4,128)(2,1)} %reshape.201), calls=%async_computation | async-start | bytes 4194304 | tf_op jit(solution)/shard_map/all_to_all | solution.py:34
  49.4 0.7 all-gather.5.cloned.1.call-update
  50.1 1.4 copy.32
  51.5 51.9 %all-to-all-done = bf16[128,3,2048]{2,1,0:T(4,128)(2,1)S(1)} async-done(((bf16[128,3,2048]{2,1,0:T(4,128)(2,1)}), bf16[128,3,2048]{2,1,0:T(4,128)(2,1)S(1)}, u32[]{:S(2)}, u32[]{:S(2)}) %all-to-all-start) | async-done | bytes 1572896 | tf_op jit(solution)/shard_map/all_to_all | solution.py:34
  103.4 1.8 stack.2
  105.2 4.8 %all-to-all-start.1 = ((bf16[4,1,768,512]{2,3,1,0:T(8,128)(2,1)}), bf16[4,1,768,512]{2,3,1,0:T(8,128)(2,1)}, u32[]{:S(2)}, u32[]{:S(2)}) async-start(bf16[4,1,768,512]{2,3,1,0:T(8,128)(2,1)} %stack.2), calls=%async_computation.1 | async-start | bytes 6291456 | tf_op jit(solution)/shard_map/all_to_all | solution.py:49
  110.0 2.5 %reshape.202 = bf16[384,2048]{1,0:T(8,128)(2,1)} reshape(bf16[128,3,2048]{2,1,0:T(4,128)(2,1)S(1)} %all-to-all-done) | data formatting | bytes 3145728 | tf_op jit(solution)/shard_map/reshape.5
  112.6 4.9 %fusion.4 = f32[384,768]{1,0:T(8,128)} fusion(bf16[384,2048]{1,0:T(8,128)(2,1)} %reshape.202, bf16[1,768,2048]{2,1,0:T(8,128)(2,1)} %all-gather.3.cloned.1.call-done), kind=kOutput, calls=%fused_computation.6 | convolution fusion | flops 1207959552 | bytes 5898240 | tf_op jit(solution)/shard_map/esd,efd->esf/dot_general | solution.py:35
  117.5 29.6 %all-to-all-done.1 = bf16[4,1,768,512]{2,3,1,0:T(8,128)(2,1)} async-done(((bf16[4,1,768,512]{2,3,1,0:T(8,128)(2,1)}), bf16[4,1,768,512]{2,3,1,0:T(8,128)(2,1)}, u32[]{:S(2)}, u32[]{:S(2)}) %all-to-all-start.1) | async-done | bytes 3145760 | tf_op jit(solution)/shard_map/all_to_all | solution.py:49
  147.1 6.3 %convolution_convert_fusion = bf16[384,2048]{1,0:T(8,128)(2,1)S(1)} fusion(bf16[768,2048]{0,1:T(8,128)(2,1)} %bitcast.11, bf16[384,2048]{1,0:T(8,128)(2,1)S(1)} %copy-done, bf16[1,768,2048]{2,1,0:T(8,128)(2,1)} %all-gather.5.cloned.1.call-done, f32[384,768]{1,0:T(8,128)} %fusion.4), kind=kOutput, calls=%fused_computation.8 | convolution fusion | flops 2418475008 | bytes 10616832 | tf_op jit(solution)/shard_map/esf,efd->esd/dot_general | solution.py:51
  153.4 1.2 reshape.207
  154.9 21.9 %all_to_all.24 = bf16[1,128,3,4,512]{4,1,2,0,3:T(8,128)(2,1)S(1)} all-to-all(bf16[1,128,3,4,512]{4,1,2,0,3:T(8,128)(2,1)S(1)} %copy.34), channel_id=1, replica_groups=mesh['rep'=4,'exp'=128] {'rep'}, dimensions={3} | all-to-all | bytes 3145728 | tf_op jit(solution)/shard_map/all_to_all | solution.py:58
  176.8 2.4 copy.35
  179.2 8.2 %all-to-all-start.3 = ((bf16[1,128,3,4,512]{4,3,2,0,1:T(4,128)(2,1)}), bf16[1,128,3,4,512]{4,3,2,0,1:T(4,128)(2,1)S(1)}, u32[]{:S(2)}, u32[]{:S(2)}) async-start(bf16[1,128,3,4,512]{4,3,2,0,1:T(4,128)(2,1)} %copy.35), calls=%async_computation.3 | async-start | bytes 3145728 | tf_op jit(solution)/shard_map/all_to_all | solution.py:57
  187.6 42.4 %all-to-all-done.3 = bf16[1,128,3,4,512]{4,3,2,0,1:T(4,128)(2,1)S(1)} async-done(((bf16[1,128,3,4,512]{4,3,2,0,1:T(4,128)(2,1)}), bf16[1,128,3,4,512]{4,3,2,0,1:T(4,128)(2,1)S(1)}, u32[]{:S(2)}, u32[]{:S(2)}) %all-to-all-start.3) | async-done | bytes 1572896 | tf_op jit(solution)/shard_map/all_to_all | solution.py:57
  230.0 0.4 reshape_transpose.3
  230.4 4.0 %gather_fusion = bf16[1024,512]{1,0:T(8,128)(2,1)S(1)} fusion(bf16[1536,512]{1,0:T(8,128)(2,1)S(1)} %reshape_transpose.3, s32[1024]{0:T(1024)S(1)} %broadcast_clamp_fusion), kind=kCustom, calls=%fused_computation | custom fusion | bytes 2101248 | tf_op jit(solution)/shard_map/gather | solution.py:65
  234.4 1.3 fusion.6
  (32 shorter events, 1.6 us)
Async XLA Ops:
  6.5 106.0 %all-gather.3.cloned.1.call-start = ((), (), s32[]{:S(2)}) async-start(), calls=%async_computation.4 | async-start | bytes 3932160 | tf_op jit(solution)/shard_map/all_gather | solution.py:38
  7.3 1.6 copy-start.2
  8.6 1.0 copy-start.1
  32.0 71.4 %all-to-all-start = ((bf16[128,3,2048]{2,1,0:T(4,128)(2,1)}), bf16[128,3,2048]{2,1,0:T(4,128)(2,1)S(1)}, u32[]{:S(2)}, u32[]{:S(2)}) async-start(bf16[128,3,2048]{2,1,0:T(4,128)(2,1)} %reshape.201), calls=%async_computation | async-start | bytes 4194304 | tf_op jit(solution)/shard_map/all_to_all | solution.py:34
  49.4 97.7 %all-gather.5.cloned.1.call-start = ((), (), s32[]{:S(2)}) async-start(), calls=%async_computation.5 | async-start | bytes 3932160 | tf_op jit(solution)/shard_map/all_gather | solution.py:44
  105.2 41.9 %all-to-all-start.1 = ((bf16[4,1,768,512]{2,3,1,0:T(8,128)(2,1)}), bf16[4,1,768,512]{2,3,1,0:T(8,128)(2,1)}, u32[]{:S(2)}, u32[]{:S(2)}) async-start(bf16[4,1,768,512]{2,3,1,0:T(8,128)(2,1)} %stack.2), calls=%async_computation.1 | async-start | bytes 6291456 | tf_op jit(solution)/shard_map/all_to_all | solution.py:49
  112.6 34.5 %copy-start = (bf16[384,2048]{1,0:T(8,128)(2,1)S(1)}, bf16[384,2048]{1,0:T(8,128)(2,1)}, u32[]{:S(2)}) copy-start(bf16[384,2048]{1,0:T(8,128)(2,1)} %reshape.202) | copy-start | bytes 4718596
  179.2 8.2 %copy-start.3 = (f32[128,8]{0,1:T(8,128)S(1)}, f32[128,8]{0,1:T(8,128)}, u32[]{:S(2)}) copy-start(f32[128,8]{0,1:T(8,128)} %param.8) | copy-start | bytes 12292
  179.2 50.8 %all-to-all-start.3 = ((bf16[1,128,3,4,512]{4,3,2,0,1:T(4,128)(2,1)}), bf16[1,128,3,4,512]{4,3,2,0,1:T(4,128)(2,1)S(1)}, u32[]{:S(2)}, u32[]{:S(2)}) async-start(bf16[1,128,3,4,512]{4,3,2,0,1:T(4,128)(2,1)} %copy.35), calls=%async_computation.3 | async-start | bytes 3145728 | tf_op jit(solution)/shard_map/all_to_all | solution.py:57
Sparse Core Ops, SparseCore 0:
  9.4 49.3 all-gather.2
  60.9 45.0 all-gather.4
